TPU v7x, 256 devices: a whole 4x4x8 slice. The times are simulated.
256 devices in a mesh: rows: 64 (over z, x, core), grp: 4 (over y).
Axes of the slice: x: 4, y: 4, z: 8, core: 2. Of those that a mesh axis runs over, the one named last changes fastest.
Arguments:
- observations: float32 [524288, 512], P(('rows', 'grp')), may hold values from -32 to 32, as said below
- sensor_ids: int32 [524288], P(('rows', 'grp')), may hold values from 0 to 127
- sensor_sigma: float32 [128], replicated, may hold values from 0.3 to 3
- buckets: int32 [524288], P(('rows', 'grp')), may hold values from 0 to 63, as said below
- prior_factor: float32 [512, 512], replicated, may hold values from -0.3 to 3, as said below
Outputs:
- whitened: float32 [524288, 512], P(('rows', 'grp'))
- info_factor: float32 [512, 512], replicated
Inputs may be any that keep to these rules, and one draw needn't show every extreme that they name: `buckets`: in each aligned block of 2048 rows every bucket index appears exactly 32 times. `observations`: rows are real-valued without further structure. `prior_factor`: upper triangular with a positive diagonal of at least 0.5.
All inputs are finite; a program needn't handle non-finite values.
Results may differ from a plain program's by a relative error of at most 0.00007.
Values sent between devices are 32-bit elements; how exact they have to be, the bound alone decides.
A program may use at most 128 MiB of HBM per device.

v0:
```python
import jax
import jax.numpy as jnp
from jax import lax
from jax.sharding import PartitionSpec as P


def matmul(left, right):
    return jnp.dot(left, right, precision=lax.Precision.HIGHEST, preferred_element_type=jnp.float32)


def outer_sum(values):
    return lax.dot_general(
        values,
        values,
        (((0,), (0,)), ((), ())),
        precision=lax.Precision.HIGHEST,
        preferred_element_type=jnp.float32,
    )


def square_form(matrix):
    return matmul(matrix.T, matrix)


def lower_inverse(lower):
    width = lower.shape[0]
    identity = jnp.eye(width, dtype=jnp.float32)
    diag_values = jnp.diagonal(lower)
    scaled_lower = lower / diag_values[:, None]
    nilpotent = identity - scaled_lower
    product = identity + nilpotent
    power = nilpotent
    reach = 2
    while reach < width:
        power = matmul(power, power)
        product = product + matmul(product, power)
        reach = reach * 2
    return product / diag_values[None, :]


def upper_factor(matrix):
    return jnp.linalg.cholesky(matrix).T


def whiten_rows(values, factor):
    inverse = lower_inverse(factor.T)
    return matmul(values, inverse.T)


def regroup_rows(values, target):
    outgoing = jnp.zeros_like(values).at[target].set(values)
    return lax.all_to_all(outgoing, "rows", split_axis=0, concat_axis=0, tiled=True)


def reduce_gram(local_gram, prior_gram, total_rows):
    summed = lax.psum(local_gram, ("rows", "grp"))
    return upper_factor(prior_gram + summed / jnp.float32(total_rows))


def shards(observations, sensor_ids, sensor_sigma, buckets, prior_factor):
    rows_dev = observations.shape[0]
    row_groups = lax.axis_size("rows")
    devices = lax.axis_size(("rows", "grp"))
    per_bucket = rows_dev // row_groups
    total_rows = rows_dev * devices
    inv_sigma = 1.0 / sensor_sigma
    matches = sensor_ids[:, None] == jnp.arange(sensor_sigma.shape[0], dtype=jnp.int32)[None, :]
    row_scale = jnp.sum(jnp.where(matches, inv_sigma[None, :], jnp.float32(0.0)), axis=1)
    scaled = observations * row_scale[:, None]
    onehot = (buckets[:, None] == jnp.arange(row_groups, dtype=jnp.int32)[None, :]).astype(
        jnp.int32
    )
    running = jnp.cumsum(onehot, axis=0)
    within = jnp.sum(onehot * running, axis=1) - 1
    target = buckets * per_bucket + within
    prior_gram = square_form(prior_factor)
    received = regroup_rows(scaled, target)
    factor = reduce_gram(outer_sum(received), prior_gram, total_rows)
    whitened = whiten_rows(received, factor)
    return (whitened, factor)


def solution(mesh):
    in_specs = (P(("rows", "grp"), None), P(("rows", "grp")), P(), P(("rows", "grp")), P())
    out_specs = (P(("rows", "grp"), None), P())
    return jax.shard_map(shards, mesh=mesh, in_specs=in_specs, out_specs=out_specs, check_vma=False)
```

profile of v0, /device:TPU:2, one launch (start us, length us, event | category | flops | bytes accessed | tf_op | source)
XLA Modules:
  0.0 560.0 jit_solution(9048692939131870598)
XLA Ops:
  7.2 0.7 broadcast_divide_fusion
  8.0 0.7 fusion.8
  8.7 18.1 %reduce-window.6 = s32[64,16,128]{2,1,0:T(8,128)S(1)} reduce-window(s32[64,16,128]{2,1,0:T(8,128)S(1)} %fusion.8, s32[]{:T(128)} %constant.151.clone.1), window={size=1x1x128 pad=0_0x0_0x127_0}, to_apply=%region_0.1 | reduce-window | flops 16646144 | bytes 1048580 | tf_op jit(solution)/shard_map/reduce-window
  27.1 0.4 copy.35
  28.1 0.6 select_reduce_fusion
  28.8 13.0 %scatter_custom_fusion = f32[2048,512]{1,0:T(8,128)} fusion(s32[2048]{0:T(1024)S(1)} %compare_select_fusion, f32[2048,512]{1,0:T(8,128)} %param.5, f32[2048]{0:T(1024)S(1)} %select_reduce_fusion, f32[]{:T(128)} %constant.149.clone.1), kind=kCustom, calls=%fused_computation.2 | custom fusion | flops 1048576 | bytes 8396804 | tf_op jit(solution)/shard_map/scatter | solution.py:51
  41.7 108.2 %all_to_all.12 = f32[64,32,512]{2,1,0:T(8,128)S(1)} all-to-all(f32[64,32,512]{2,1,0:T(8,128)} %bitcast.84), channel_id=1, replica_groups=mesh['rows'=64,'grp'=4] {'rows'}, dimensions={0} | all-to-all | bytes 8388608 | tf_op jit(solution)/shard_map/all_to_all | solution.py:52
  149.9 2.0 copy-done.1
  152.0 8.0 %convolution_bitcast_fusion = f32[512,512]{0,1:T(8,128)} fusion(f32[64,32,512]{2,1,0:T(8,128)S(1)} %all_to_all.12), kind=kOutput, calls=%fused_computation.17 | convolution fusion | flops 6442450944 | bytes 5242880 | tf_op jit(solution)/shard_map/dot_general | solution.py:12
  160.0 252.4 %all-reduce.3.cloned.1.call-done = f32[512,512]{0,1:T(8,128)} async-done(((f32[512,512]{0,1:T(8,128)}), f32[512,512]{0,1:T(8,128)}) %all-reduce.3.cloned.1.call-update) | async-done | bytes 1048592 | tf_op jit(solution)/shard_map/psum | solution.py:56
  412.5 3.1 convolution_add_fusion.8
  415.6 0.3 copy.31
  416.2 1.0 copy-done.3
  417.1 12.2 %cholesky.104 = f32[128,128]{1,0:T(8,128)S(1)} custom-call(f32[128,128]{1,0:T(8,128)S(1)} %cholesky.266), custom_call_target="Cholesky" | custom-call | tf_op jit(solution)/shard_map/jit(cholesky)/cholesky | solution.py:42
  429.5 9.8 %custom-call.27 = f32[1,128,128]{1,2,0:T(8,128)S(1)} custom-call(f32[1,128,128]{2,1,0:T(8,128)S(1)} %get-tuple-element.19), custom_call_target="InvertDiagBlocksLowerTriangular" | custom-call | tf_op jit(solution)/shard_map/jit(cholesky)/cholesky | solution.py:42
  439.3 1.2 constant_dynamic-update-slice_fusion.2
  440.6 1.3 convolution_subtract_fusion
  441.9 11.7 %cholesky.217 = f32[128,128]{1,0:T(8,128)S(1)} custom-call(f32[128,128]{1,0:T(8,128)S(1)} %cholesky.270), custom_call_target="Cholesky" | custom-call | tf_op jit(solution)/shard_map/jit(cholesky)/cholesky | solution.py:42
  453.6 9.8 %custom-call.28 = f32[1,128,128]{1,2,0:T(8,128)S(1)} custom-call(f32[1,128,128]{2,1,0:T(8,128)S(1)} %get-tuple-element.16), custom_call_target="InvertDiagBlocksLowerTriangular" | custom-call | tf_op jit(solution)/shard_map/jit(cholesky)/cholesky | solution.py:42
  463.4 0.3 convolution_dynamic-update-slice_fusion
  463.7 1.3 convolution_subtract_fusion.1
  465.0 11.9 %cholesky.238 = f32[128,128]{1,0:T(8,128)S(1)} custom-call(f32[128,128]{1,0:T(8,128)S(1)} %cholesky.275), custom_call_target="Cholesky" | custom-call | tf_op jit(solution)/shard_map/jit(cholesky)/cholesky | solution.py:42
  476.9 0.7 compare_reduce_fusion.1
  477.6 9.8 %custom-call.29 = f32[1,128,128]{1,2,0:T(8,128)S(1)} custom-call(f32[1,128,128]{2,1,0:T(8,128)S(1)} %get-tuple-element.13), custom_call_target="InvertDiagBlocksLowerTriangular" | custom-call | tf_op jit(solution)/shard_map/jit(cholesky)/cholesky | solution.py:42
  487.6 1.2 convolution_subtract_fusion.2
  488.9 11.7 %cholesky.255 = f32[128,128]{1,0:T(8,128)S(1)} custom-call(f32[128,128]{1,0:T(8,128)S(1)} %convolution_subtract_fusion.2), custom_call_target="Cholesky" | custom-call | tf_op jit(solution)/shard_map/jit(cholesky)/cholesky | solution.py:42
  500.6 0.6 compare_reduce_fusion
  501.3 0.7 compare_reduce_fusion.2
  504.6 1.2 fusion.65
  505.8 4.7 gather_fusion
  510.5 2.1 fusion.20
  512.6 3.0 convolution_add_fusion.7
  515.6 1.8 fusion.21
  517.4 2.5 copy.32
  520.0 1.8 fusion.22
  521.8 1.8 convolution_add_fusion.6
  523.7 1.8 fusion.23
  525.5 1.8 convolution_add_fusion.5
  527.4 2.3 fusion.24
  529.7 1.9 convolution_add_fusion.4
  531.5 1.8 fusion.25
  533.4 1.8 convolution_add_fusion.3
  535.2 1.8 fusion.26
  537.1 1.9 convolution_add_fusion.2
  538.9 1.8 fusion.27
  540.8 2.0 convolution_add_fusion.1
  542.8 1.9 fusion.4
  544.7 8.3 %fusion.28 = f32[2048,512]{1,0:T(8,128)} fusion(f32[2048,512]{1,0:T(8,128)S(1)} %bitcast.82, f32[512,512]{1,0:T(8,128)S(1)} %fusion.4), kind=kOutput, calls=%fused_computation.77 | convolution fusion | flops 6442450944 | bytes 9437184 | tf_op jit(solution)/shard_map/dot_general | solution.py:8
  (31 shorter events, 1.7 us)
Async XLA Ops:
  7.2 405.3 %copy-start = (f32[512,512]{1,0:T(8,128)S(1)}, f32[512,512]{1,0:T(8,128)}, u32[]{:S(2)}) copy-start(f32[512,512]{1,0:T(8,128)} %param.9) | copy-start | bytes 3145732
  7.2 20.7 %copy-start.5 = (s32[2048]{0:T(1024)S(1)}, s32[2048]{0:T(1024)}, u32[]{:S(2)}) copy-start(s32[2048]{0:T(1024)} %param.8) | copy-start | bytes 24580
  7.2 20.9 %copy-start.6 = (s32[2048]{0:T(1024)S(1)}, s32[2048]{0:T(1024)}, u32[]{:S(2)}) copy-start(s32[2048]{0:T(1024)} %param.6) | copy-start | bytes 24580
  7.2 405.3 %all-reduce.3.cloned.1.call-start = ((), (), s32[]{:S(2)}) async-start(), calls=%async_computation.1 | async-start | bytes 2097152 | tf_op jit(solution)/shard_map/psum | solution.py:56
  149.9 2.0 copy-start.1
  416.1 1.0 copy-start.3
  515.6 6.2 %copy-start.4 = (f32[512,512]{1,0:T(8,128)S(1)}, f32[512,512]{1,0:T(8,128)}, u32[]{:S(2)}) copy-start(f32[512,512]{1,0:T(8,128)} %convolution_add_fusion.7) | copy-start | bytes 3145732
  540.8 3.9 copy-start.2
Sparse Core Ops, SparseCore 0:
  160.1 252.2 all-reduce.2
where the time goes:
time: 565 us; the launch traced here: 560 us
  waiting for transfers between devices  252 us (45%)
  other arithmetic  114 us (20%)
  blocking collectives  108 us (19%)
  matrix products  56.4 us (10%)
  between operations  17.1 us (3%)
  local copies, waits for them, and re-layouts  11.4 us (2%)
    psum x1, waiting for transfers between devices, reduce_gram(): summed = lax.psum(local_gram, ('rows', 'grp'))  252 us
    all_to_all x1, blocking collectives, regroup_rows(): lax.all_to_all(outgoing, 'rows', split_axis=0, concat_axis=0, tiled=True)  108 us
    another operation x14, other arithmetic, upper_factor(): return jnp.linalg.cholesky(matrix).T  79.1 us
    dot_general x18, matrix products, matmul(): jnp.dot(left, right, precision=lax.Precision.HIGHEST, preferred_element_t...  42.9 us
    another operation x3, other arithmetic  18.5 us
    scatter x1, other arithmetic, regroup_rows(): outgoing = jnp.zeros_like(values).at[target].set(values)  13 us
  transfers between devices with their start and end apart: 1, of which 1 were waited for; matrix products, arithmetic and copies ran while one was open for 0% of the time, Pallas kernels for 0%

commit v1 on v0

--- a/solution.py
+++ b/solution.py
@@ -53,7 +53,7 @@
 
 
 def reduce_gram(local_gram, prior_gram, total_rows):
-    summed = lax.psum(local_gram, ("rows", "grp"))
+    summed = lax.psum(lax.psum(local_gram, "rows"), "grp")
     return upper_factor(prior_gram + summed / jnp.float32(total_rows))
 
 

time: 565 us -> 545 us (0.965)
  waiting for transfers between devices: 252 us -> 233 us
    psum x1 -> x2, waiting for transfers between devices: 252 us -> 233 us  [reduce_gram(): summed = lax.psum(lax.psum(local_gram, 'rows'), 'grp')]
  transfers between devices with their start and end apart: 1 -> 2, of which waited for: 1 -> 2; matrix products, arithmetic and copies ran while one was open for 0% -> 0% of each run, Pallas kernels for 0% -> 0%
where the time goes in v1:
time: 545 us; the launch traced here: 541 us
  waiting for transfers between devices  233 us (43%)
  other arithmetic  114 us (21%)
  blocking collectives  109 us (20%)
  matrix products  56.3 us (10%)
  between operations  17.4 us (3%)
  local copies, waits for them, and re-layouts  11.2 us (2%)
    psum x2, waiting for transfers between devices, reduce_gram(): summed = lax.psum(lax.psum(local_gram, 'rows'), 'grp')  233 us
    all_to_all x1, blocking collectives, regroup_rows(): lax.all_to_all(outgoing, 'rows', split_axis=0, concat_axis=0, tiled=True)  109 us
    another operation x14, other arithmetic, upper_factor(): return jnp.linalg.cholesky(matrix).T  79 us
    dot_general x18, matrix products, matmul(): jnp.dot(left, right, precision=lax.Precision.HIGHEST, preferred_element_t...  42.8 us
    another operation x3, other arithmetic  18.5 us
    scatter x1, other arithmetic, regroup_rows(): outgoing = jnp.zeros_like(values).at[target].set(values)  13 us
  transfers between devices with their start and end apart: 2, of which 2 were waited for; matrix products, arithmetic and copies ran while one was open for 0% of the time, Pallas kernels for 0%

profile of v1, /device:TPU:2, one launch (start us, length us, event | category | flops | bytes accessed | tf_op | source)
XLA Modules:
  0.0 540.7 jit_solution(14596436237308876592)
XLA Ops:
  7.2 0.7 broadcast_divide_fusion
  8.0 0.7 fusion.8
  8.7 18.1 %reduce-window.6 = s32[64,16,128]{2,1,0:T(8,128)S(1)} reduce-window(s32[64,16,128]{2,1,0:T(8,128)S(1)} %fusion.8, s32[]{:T(128)} %constant.151.clone.1), window={size=1x1x128 pad=0_0x0_0x127_0}, to_apply=%region_0.1 | reduce-window | flops 16646144 | bytes 1048580 | tf_op jit(solution)/shard_map/reduce-window
  27.1 0.4 copy.35
  28.1 0.6 select_reduce_fusion
  28.8 13.0 %scatter_custom_fusion = f32[2048,512]{1,0:T(8,128)} fusion(s32[2048]{0:T(1024)S(1)} %compare_select_fusion, f32[2048,512]{1,0:T(8,128)} %param.5, f32[2048]{0:T(1024)S(1)} %select_reduce_fusion, f32[]{:T(128)} %constant.149.clone.1), kind=kCustom, calls=%fused_computation.2 | custom fusion | flops 1048576 | bytes 8396804 | tf_op jit(solution)/shard_map/scatter | solution.py:51
  41.7 108.7 %all_to_all.12 = f32[64,32,512]{2,1,0:T(8,128)S(1)} all-to-all(f32[64,32,512]{2,1,0:T(8,128)} %bitcast.84), channel_id=1, replica_groups=mesh['rows'=64,'grp'=4] {'rows'}, dimensions={0} | all-to-all | bytes 8388608 | tf_op jit(solution)/shard_map/all_to_all | solution.py:52
  150.5 2.0 copy-done.1
  152.5 8.0 %convolution_bitcast_fusion = f32[512,512]{0,1:T(8,128)} fusion(f32[64,32,512]{2,1,0:T(8,128)S(1)} %all_to_all.12), kind=kOutput, calls=%fused_computation.17 | convolution fusion | flops 6442450944 | bytes 5242880 | tf_op jit(solution)/shard_map/dot_general | solution.py:12
  160.8 181.5 %all-reduce.4.cloned.1.call-done = f32[512,512]{0,1:T(8,128)} async-done(((f32[512,512]{0,1:T(8,128)}), f32[512,512]{0,1:T(8,128)}) %all-reduce.4.cloned.1.call-update) | async-done | bytes 1048592 | tf_op jit(solution)/shard_map/psum | solution.py:56
  342.3 51.0 %all-reduce.6.cloned.1.call-done = f32[512,512]{0,1:T(8,128)} async-done(((f32[512,512]{0,1:T(8,128)}), f32[512,512]{0,1:T(8,128)}) %all-reduce.6.cloned.1.call-update) | async-done | bytes 1048592 | tf_op jit(solution)/shard_map/psum | solution.py:56
  393.3 3.1 convolution_add_fusion.8
  396.4 0.3 copy.31
  397.0 1.0 copy-done.3
  398.0 11.7 %cholesky.104 = f32[128,128]{1,0:T(8,128)S(1)} custom-call(f32[128,128]{1,0:T(8,128)S(1)} %cholesky.266), custom_call_target="Cholesky" | custom-call | tf_op jit(solution)/shard_map/jit(cholesky)/cholesky | solution.py:42
  409.9 9.8 %custom-call.27 = f32[1,128,128]{1,2,0:T(8,128)S(1)} custom-call(f32[1,128,128]{2,1,0:T(8,128)S(1)} %get-tuple-element.19), custom_call_target="InvertDiagBlocksLowerTriangular" | custom-call | tf_op jit(solution)/shard_map/jit(cholesky)/cholesky | solution.py:42
  419.7 1.2 constant_dynamic-update-slice_fusion.2
  420.9 1.3 convolution_subtract_fusion
  422.2 12.1 %cholesky.217 = f32[128,128]{1,0:T(8,128)S(1)} custom-call(f32[128,128]{1,0:T(8,128)S(1)} %cholesky.270), custom_call_target="Cholesky" | custom-call | tf_op jit(solution)/shard_map/jit(cholesky)/cholesky | solution.py:42
  434.3 9.8 %custom-call.28 = f32[1,128,128]{1,2,0:T(8,128)S(1)} custom-call(f32[1,128,128]{2,1,0:T(8,128)S(1)} %get-tuple-element.16), custom_call_target="InvertDiagBlocksLowerTriangular" | custom-call | tf_op jit(solution)/shard_map/jit(cholesky)/cholesky | solution.py:42
  444.4 1.3 convolution_subtract_fusion.1
  445.7 11.7 %cholesky.238 = f32[128,128]{1,0:T(8,128)S(1)} custom-call(f32[128,128]{1,0:T(8,128)S(1)} %cholesky.275), custom_call_target="Cholesky" | custom-call | tf_op jit(solution)/shard_map/jit(cholesky)/cholesky | solution.py:42
  457.5 0.7 compare_reduce_fusion.1
  458.2 9.8 %custom-call.29 = f32[1,128,128]{1,2,0:T(8,128)S(1)} custom-call(f32[1,128,128]{2,1,0:T(8,128)S(1)} %get-tuple-element.13), custom_call_target="InvertDiagBlocksLowerTriangular" | custom-call | tf_op jit(solution)/shard_map/jit(cholesky)/cholesky | solution.py:42
  468.2 1.2 convolution_subtract_fusion.2
  469.5 11.9 %cholesky.255 = f32[128,128]{1,0:T(8,128)S(1)} custom-call(f32[128,128]{1,0:T(8,128)S(1)} %convolution_subtract_fusion.2), custom_call_target="Cholesky" | custom-call | tf_op jit(solution)/shard_map/jit(cholesky)/cholesky | solution.py:42
  481.4 0.6 compare_reduce_fusion
  482.0 0.7 compare_reduce_fusion.2
  485.3 1.2 fusion.65
  486.5 4.5 gather_fusion
  491.0 2.1 fusion.20
  493.1 3.0 convolution_add_fusion.7
  496.1 1.8 fusion.21
  497.9 2.5 copy.32
  500.5 1.8 fusion.22
  502.3 1.8 convolution_add_fusion.6
  504.2 1.8 fusion.23
  506.0 1.8 convolution_add_fusion.5
  507.9 2.1 fusion.24
  510.0 1.8 convolution_add_fusion.4
  511.8 1.8 fusion.25
  513.7 1.8 convolution_add_fusion.3
  515.5 1.8 fusion.26
  517.4 1.8 convolution_add_fusion.2
  519.2 1.8 fusion.27
  521.1 2.1 convolution_add_fusion.1
  523.2 1.9 fusion.4
  525.1 8.3 %fusion.28 = f32[2048,512]{1,0:T(8,128)} fusion(f32[2048,512]{1,0:T(8,128)S(1)} %bitcast.82, f32[512,512]{1,0:T(8,128)S(1)} %fusion.4), kind=kOutput, calls=%fused_computation.77 | convolution fusion | flops 6442450944 | bytes 9437184 | tf_op jit(solution)/shard_map/dot_general | solution.py:8
  (34 shorter events, 2.2 us)
Async XLA Ops:
  7.2 386.2 %copy-start = (f32[512,512]{1,0:T(8,128)S(1)}, f32[512,512]{1,0:T(8,128)}, u32[]{:S(2)}) copy-start(f32[512,512]{1,0:T(8,128)} %param.9) | copy-start | bytes 3145732
  7.2 20.7 %copy-start.5 = (s32[2048]{0:T(1024)S(1)}, s32[2048]{0:T(1024)}, u32[]{:S(2)}) copy-start(s32[2048]{0:T(1024)} %param.8) | copy-start | bytes 24580
  7.2 20.9 %copy-start.6 = (s32[2048]{0:T(1024)S(1)}, s32[2048]{0:T(1024)}, u32[]{:S(2)}) copy-start(s32[2048]{0:T(1024)} %param.6) | copy-start | bytes 24580
  7.2 335.1 %all-reduce.4.cloned.1.call-start = ((), (), s32[]{:S(2)}) async-start(), calls=%async_computation.1 | async-start | bytes 2097152 | tf_op jit(solution)/shard_map/psum | solution.py:56
  150.5 2.0 copy-start.1
  160.5 232.8 %all-reduce.6.cloned.1.call-start = ((), (), s32[]{:S(2)}) async-start(), calls=%async_computation.2 | async-start | bytes 2097152 | tf_op jit(solution)/shard_map/psum | solution.py:56
  397.0 1.0 copy-start.3
  496.1 6.2 %copy-start.4 = (f32[512,512]{1,0:T(8,128)S(1)}, f32[512,512]{1,0:T(8,128)}, u32[]{:S(2)}) copy-start(f32[512,512]{1,0:T(8,128)} %convolution_add_fusion.7) | copy-start | bytes 3145732
  521.1 4.0 copy-start.2
Sparse Core Ops, SparseCore 0:
  160.7 181.6 all-reduce.3
  344.8 48.4 all-reduce.5
